TPU v7x, 128 devices: a whole 4x4x4 slice. The times are simulated.
128 devices in a mesh: dp: 16 (over x, z), blk: 8 (over y, core).
Axes of the slice: x: 4, y: 4, z: 4, core: 2. Of those that a mesh axis runs over, the one named last changes fastest.
Arguments:
- entity_table: float32 [262144, 400], P(('dp', 'blk')), may hold values from -1.8 to 1.8
- adagrad_sum: float32 [262144], P(('dp', 'blk')), may hold values from 0.0001 to 0.001
- relations: float32 [7424, 400], replicated, may hold values from -1.8 to 1.8
- owner_map: int32 [262144], replicated, may hold values from 0 to 262143, as said below
- head_ids: int32 [16384], P(('dp', 'blk')), may hold values from 0 to 262143, as said below
- rel_ids: int32 [16384], P(('dp', 'blk')), may hold values from 0 to 7423
- tail_ids: int32 [16384], P(('dp', 'blk')), may hold values from 0 to 262143, as said below
- neg_ids: int32 [65536], P(('dp', 'blk')), may hold values from 0 to 262143, as said below
Outputs:
- new_table: float32 [262144, 400], P(('dp', 'blk'))
- new_sum: float32 [262144], P(('dp', 'blk'))
Inputs may be any that keep to these rules, and one draw needn't show every extreme that they name: `owner_map`: A permutation: every storage position appears once. The owner of position p is device p // 2048. `head_ids`: among the 128 heads, 128 tails and 512 negatives of one device taken together, at most 12 are stored on any one owner; in every draw 16 owners receive exactly 12 from every device. `tail_ids`: counted together with the heads and negatives of the same device, as stated for head_ids. `neg_ids`: counted together with the heads and tails of the same device, as stated for head_ids.
All inputs are finite; a program needn't handle non-finite values.
Results may differ from a plain program's by a relative error of at most 0.00005.
Values sent between devices are 32-bit elements; how exact they have to be, the bound alone decides.
A program may use at most 128 MiB of HBM per device.

v0:
```python
import jax
import jax.numpy as jnp
from jax import lax
from jax.sharding import PartitionSpec as P

MARGIN = 10.0
EPSILON = 1e-05
LEARNING_RATE = 0.1


def negative_terms(queries, neg_block, weight):
    query_sq = jnp.sum(queries * queries, axis=1)
    block_sq = jnp.sum(neg_block * neg_block, axis=1)
    inner_prod = jnp.dot(
        queries, neg_block.T, precision=lax.Precision.HIGHEST, preferred_element_type=jnp.float32
    )
    distance = jnp.sqrt(query_sq[:, None] + block_sq[None, :] - 2.0 * inner_prod + EPSILON)
    coefficient = -jax.nn.sigmoid(MARGIN - distance) / (weight * distance)
    grad_query = queries * jnp.sum(coefficient, axis=1)[:, None] - jnp.dot(
        coefficient, neg_block, precision=lax.Precision.HIGHEST, preferred_element_type=jnp.float32
    )
    grad_block = neg_block * jnp.sum(coefficient, axis=0)[:, None] - jnp.dot(
        coefficient.T, queries, precision=lax.Precision.HIGHEST, preferred_element_type=jnp.float32
    )
    return (grad_query, grad_block)


def send_requests(requests):
    return lax.all_to_all(requests, ("dp", "blk"), split_axis=0, concat_axis=0, tiled=True)


def move_rows(payload):
    return lax.all_to_all(payload, ("dp", "blk"), split_axis=0, concat_axis=0, tiled=True)


def on_device(
    entity_table, adagrad_sum, relations, owner_map, head_ids, rel_ids, tail_ids, neg_ids
):
    dp_count = lax.axis_size("dp")
    blk_count = lax.axis_size("blk")
    owner_count = dp_count * blk_count
    rows_here, width = entity_table.shape
    edge_count = head_ids.shape[0]
    neg_count = neg_ids.shape[0]
    request_count = 2 * edge_count + neg_count
    capacity = max(2, 2 * request_count // owner_count)
    wanted = jnp.concatenate([head_ids, tail_ids, neg_ids])
    position = owner_map[wanted]
    owner_of = position // rows_here
    local_row = position % rows_here
    onehot = (owner_of[:, None] == jnp.arange(owner_count, dtype=jnp.int32)[None, :]).astype(
        jnp.int32
    )
    before = jnp.cumsum(onehot, axis=0) - onehot
    rank_in = jnp.sum(before * onehot, axis=1)
    slot_of = owner_of * capacity + rank_in
    requests = jnp.zeros((owner_count * capacity,), jnp.int32).at[slot_of].set(local_row)
    requests = requests.reshape(owner_count, capacity)
    asked_rows = send_requests(requests)
    served = entity_table[asked_rows]
    fetched = move_rows(served).reshape(owner_count * capacity, width)[slot_of]
    head_rows = fetched[:edge_count]
    tail_rows = fetched[edge_count : 2 * edge_count]
    neg_block = fetched[2 * edge_count :]
    queries = head_rows + relations[rel_ids]
    residue = queries - tail_rows
    pos_dist = jnp.sqrt(jnp.sum(residue * residue, axis=1) + EPSILON)
    grad_pos = (jax.nn.sigmoid(pos_dist - MARGIN) / pos_dist)[:, None] * residue
    weight = float(blk_count * neg_count)
    part_query, part_block = negative_terms(
        queries, lax.all_gather(neg_block, "blk", axis=0, tiled=True), weight
    )
    block_grad = lax.psum_scatter(part_block, "blk", scatter_dimension=0, tiled=True)
    gradients = jnp.concatenate([grad_pos + part_query, -grad_pos, block_grad])
    outgoing = jnp.zeros((owner_count * capacity, width), jnp.float32).at[slot_of].set(gradients)
    incoming = move_rows(outgoing.reshape(owner_count, capacity, width))
    summed = (
        jnp.zeros_like(entity_table).at[asked_rows.reshape(-1)].add(incoming.reshape(-1, width))
    )
    new_sum = adagrad_sum + jnp.mean(summed * summed, axis=1)
    new_table = entity_table - LEARNING_RATE * summed / jnp.sqrt(new_sum)[:, None]
    return (new_table, new_sum)


def solution(mesh):
    return jax.shard_map(
        on_device,
        mesh=mesh,
        in_specs=(
            P(("dp", "blk"), None),
            P(("dp", "blk")),
            P(),
            P(),
            P(("dp", "blk")),
            P(("dp", "blk")),
            P(("dp", "blk")),
            P(("dp", "blk")),
        ),
        out_specs=(P(("dp", "blk"), None), P(("dp", "blk"))),
        check_vma=False,
    )
```

profile of v0, /device:TPU:1, one launch (start us, length us, event | category | flops | bytes accessed | tf_op | source)
XLA Modules:
  0.0 335.3 jit_solution(6407851075444210870)
XLA Ops:
  7.2 0.8 fusion.20
  8.0 0.4 copy-done
  8.4 4.5 %gather_fusion = s32[768]{0:T(1024)S(1)} fusion(s32[262144]{0:T(1024)S(1)} %copy-done, s32[1024]{0:T(1024)S(1)} %pad_clamp_fusion.3), kind=kCustom, calls=%fused_computation | custom fusion | bytes 9216 | tf_op jit(solution)/shard_map/gather | solution.py:48
  12.9 0.1 copy.29
  13.1 0.2 fusion.8
  13.4 0.3 fusion.11
  13.8 3.4 %scatter_custom_fusion = s32[1536]{0:T(1024)S(1)} fusion(s32[768]{0:T(1024)S(1)} %fusion.21, s32[768]{0:T(1024)S(1)} %get-tuple-element.15, s32[]{:T(128)} %constant.22.clone.1), kind=kCustom, calls=%fused_computation.64 | custom fusion | bytes 6148 | tf_op jit(solution)/shard_map/scatter | solution.py:57
  17.2 0.7 all_to_all.14
  17.9 11.5 %all-to-all-start = ((s32[128,1,12]{2,1,0:T(1,128)}), s32[128,1,12]{2,1,0:T(1,128)S(1)}, u32[]{:S(2)}, u32[]{:S(2)}) async-start(s32[128,1,12]{2,1,0:T(1,128)} %bitcast.7), calls=%async_computation | async-start | bytes 131072 | tf_op jit(solution)/shard_map/all_to_all | solution.py:29
  29.4 5.1 %copy.39 = f32[2048,400]{1,0:T(8,128)} copy(f32[2048,400]{0,1:T(8,128)} %param.8) | data formatting | bytes 6553600 | tf_op args[0]
  34.4 4.4 %all-to-all-done = s32[128,1,12]{2,1,0:T(1,128)S(1)} async-done(((s32[128,1,12]{2,1,0:T(1,128)}), s32[128,1,12]{2,1,0:T(1,128)S(1)}, u32[]{:S(2)}, u32[]{:S(2)}) %all-to-all-start) | async-done | bytes 6176 | tf_op jit(solution)/shard_map/all_to_all | solution.py:29
  38.8 0.1 reshape.314
  38.9 7.9 %gather_fusion.1 = f32[1536,400]{1,0:T(8,128)} fusion(f32[2048,400]{1,0:T(8,128)} %copy.39, s32[2048]{0:T(1024)S(1)} %pad_clamp_fusion), kind=kCustom, calls=%fused_computation.1 | custom fusion | bytes 4921344 | tf_op jit(solution)/shard_map/gather | solution.py:60
  46.8 4.6 %reshape.313 = f32[128,12,400]{2,1,0:T(8,128)} reshape(f32[1536,400]{1,0:T(8,128)} %gather_fusion.1) | data formatting | bytes 4915200 | tf_op jit(solution)/shard_map/gather | solution.py:60
  51.4 5.9 %all-to-all-start.1 = ((f32[128,12,400]{2,1,0:T(8,128)}), f32[128,12,400]{2,1,0:T(8,128)}, u32[]{:S(2)}, u32[]{:S(2)}) async-start(f32[128,12,400]{2,1,0:T(8,128)} %reshape.313), calls=%async_computation.1 | async-start | bytes 8388608 | tf_op jit(solution)/shard_map/all_to_all | solution.py:33
  57.3 52.5 %all-to-all-done.1 = f32[128,12,400]{2,1,0:T(8,128)} async-done(((f32[128,12,400]{2,1,0:T(8,128)}), f32[128,12,400]{2,1,0:T(8,128)}, u32[]{:S(2)}, u32[]{:S(2)}) %all-to-all-start.1) | async-done | bytes 2457632 | tf_op jit(solution)/shard_map/all_to_all | solution.py:33
  109.8 4.6 %reshape.301 = f32[1536,400]{1,0:T(8,128)} reshape(f32[128,12,400]{2,1,0:T(8,128)} %all-to-all-done.1) | data formatting | bytes 4915200 | tf_op jit(solution)/shard_map/reshape | solution.py:61
  114.4 4.7 %gather_fusion.2 = f32[768,400]{1,0:T(8,128)S(1)} fusion(f32[1536,400]{1,0:T(8,128)} %reshape.301, s32[1024]{0:T(1024)S(1)} %pad_clamp_fusion.2), kind=kCustom, calls=%fused_computation.2 | custom fusion | bytes 2460672 | tf_op jit(solution)/shard_map/gather | solution.py:61
  119.1 1.2 copy.43
  120.4 0.2 reduce-scatter.2.cloned.1.call-start
  120.6 14.2 %copy.34 = f32[7424,400]{1,0:T(8,128)} copy(f32[7424,400]{0,1:T(8,128)} %param.10) | data formatting | bytes 23756800 | tf_op args[2]
  134.8 6.5 %gather_fusion.3 = f32[128,400]{1,0:T(8,128)S(1)} fusion(f32[7424,400]{1,0:T(8,128)} %copy.34, s32[1024]{0:T(1024)S(1)} %pad_clamp_fusion.1), kind=kCustom, calls=%fused_computation.3 | custom fusion | bytes 410112 | tf_op jit(solution)/shard_map/gather | solution.py:65
  141.3 0.1 copy.35
  141.5 0.1 copy.41
  141.6 0.1 copy.42
  141.9 18.3 %all-gather.2.cloned.1.call-done = f32[4096,400]{0,1:T(8,128)} async-done(((f32[512,400]{0,1:T(8,128)}), f32[4096,400]{0,1:T(8,128)}) %all-gather.2.cloned.1.call-update) | async-done | bytes 6553616 | tf_op jit(solution)/shard_map/all_gather | solution.py:71
  160.3 3.6 %multiply_reduce_fusion = f32[4096]{0:T(1024)S(1)} fusion(f32[4096,400]{0,1:T(8,128)} %all-gather.2.cloned.1.call-done), kind=kLoop, calls=%fused_computation.8 | loop fusion | flops 3272704 | bytes 6569984 | tf_op jit(solution)/shard_map/reduce_sum | solution.py:13
  163.9 1.1 copy-done.3
  165.0 5.5 %fusion.23 = (f32[128]{0:T(128)S(1)}, f32[4096]{0:T(1024)S(1)}, f32[128,4096]{1,0:T(8,128)S(1)}) fusion(f32[128,400]{0,1:T(8,128)S(1)} %get-tuple-element.12, f32[4096,400]{0,1:T(8,128)S(1)} %copy-done.3, f32[4096]{0:T(1024)S(1)} %multiply_reduce_fusion, f32[128]{0:T(128)S(1)} %multiply_reduce_fusion.2), kind=kOutput, calls=%fused_computation.73 | convolution fusion | flops 2523394048 | bytes 8889344 | tf_op jit(solution)/shard_map/dot_general | solution.py:14
  170.5 7.6 %multiply_subtract_fusion = f32[4096,400]{0,1:T(8,128)} fusion(f32[4096,400]{0,1:T(8,128)S(1)} %copy-done.3, f32[128,4096]{1,0:T(8,128)S(1)} %get-tuple-element.17, f32[128,400]{0,1:T(8,128)S(1)} %get-tuple-element.12, f32[4096]{0:T(1024)S(1)} %get-tuple-element.7), kind=kOutput, calls=%fused_computation.7 | convolution fusion | flops 2519859200 | bytes 15425536 | tf_op jit(solution)/shard_map/dot_general | solution.py:22
  178.2 7.6 %fusion.7 = f32[128,400]{0,1:T(8,128)S(1)} fusion(f32[128,4096]{1,0:T(8,128)S(1)} %get-tuple-element.17, f32[4096,400]{0,1:T(8,128)} %all-gather.2.cloned.1.call-done, f32[128,400]{0,1:T(8,128)S(1)} %get-tuple-element.12, f32[128,400]{0,1:T(8,128)S(1)} %get-tuple-element.11, f32[128]{0:T(128)S(1)} %get-tuple-element.6, f32[128]{0:T(128)S(1)} %multiply_divide_fusion.1), kind=kOutput, calls=%fused_computation.22 | convolution fusion | flops 2516787200 | bytes 9266176 | tf_op jit(solution)/shard_map/dot_general | solution.py:19
  185.8 35.3 %reduce-scatter.2.cloned.1.call-done = f32[512,400]{0,1:T(8,128)} async-done(((f32[4096,400]{0,1:T(8,128)}), f32[512,400]{0,1:T(8,128)}) %reduce-scatter.2.cloned.1.call-update) | async-done | bytes 819216 | tf_op jit(solution)/shard_map/reduce_scatter | solution.py:73
  221.1 1.2 pad_maximum_fusion
  222.3 1.6 copy.38
  223.9 8.0 %scatter_custom_fusion.1 = f32[1536,400]{1,0:T(8,128)} fusion(s32[768]{0:T(1024)S(1)} %fusion.21, f32[768,400]{1,0:T(8,128)} %copy.38, f32[]{:T(128)} %constant.21.clone.1), kind=kCustom, calls=%fused_computation.18 | custom fusion | bytes 2458112 | tf_op jit(solution)/shard_map/scatter | solution.py:75
  232.0 4.6 %reshape.302 = f32[128,12,400]{2,1,0:T(8,128)} reshape(f32[1536,400]{1,0:T(8,128)} %scatter_custom_fusion.1) | data formatting | bytes 4915200 | tf_op jit(solution)/shard_map/reshape | solution.py:76
  236.5 8.9 %all-to-all-start.2 = ((f32[128,12,400]{2,1,0:T(8,128)}), f32[128,12,400]{2,1,0:T(8,128)}, u32[]{:S(2)}, u32[]{:S(2)}) async-start(f32[128,12,400]{2,1,0:T(8,128)} %reshape.302), calls=%async_computation.3 | async-start | bytes 8388608 | tf_op jit(solution)/shard_map/all_to_all | solution.py:33
  245.4 0.5 broadcast.247
  245.9 0.8 reduce.9
  246.7 0.1 reshape.300
  246.9 51.1 %all-to-all-done.2 = f32[128,12,400]{2,1,0:T(8,128)} async-done(((f32[128,12,400]{2,1,0:T(8,128)}), f32[128,12,400]{2,1,0:T(8,128)}, u32[]{:S(2)}, u32[]{:S(2)}) %all-to-all-start.2) | async-done | bytes 2457632 | tf_op jit(solution)/shard_map/all_to_all | solution.py:33
  297.9 4.6 %reshape.356 = f32[1536,400]{1,0:T(8,128)} reshape(f32[128,12,400]{2,1,0:T(8,128)} %all-to-all-done.2) | data formatting | bytes 4915200 | tf_op jit(solution)/shard_map/reshape | solution.py:78
  302.5 12.4 %scatter_custom_fusion.2 = f32[2048,400]{1,0:T(8,128)} fusion(s32[1536]{0:T(1024)S(1)} %fusion.13, f32[1536,400]{1,0:T(8,128)} %reshape.356, f32[]{:T(128)} %constant.21.clone.1), kind=kCustom, calls=%fused_computation.16 | custom fusion | flops 614400 | bytes 3277312 | tf_op jit(solution)/shard_map/scatter-add | solution.py:78
  314.9 2.7 multiply_reduce_fusion.1
  317.6 0.6 fusion.24
  318.2 0.1 copy-done.2
  318.4 4.9 %divide_subtract_fusion = f32[2048,400]{1,0:T(8,128)} fusion(f32[2048,400]{1,0:T(8,128)S(1)} %copy-done.2, f32[2048,400]{1,0:T(8,128)} %scatter_custom_fusion.2, f32[2048]{0:T(1024)S(1)} %get-tuple-element.8), kind=kLoop, calls=%fused_computation.13 | loop fusion | flops 2457600 | bytes 9838592 | tf_op jit(solution)/shard_map/sub | solution.py:81
  323.3 5.2 %copy.40 = f32[2048,400]{0,1:T(8,128)} copy(f32[2048,400]{1,0:T(8,128)} %divide_subtract_fusion) | data formatting | bytes 6553600
  (32 shorter events, 0.7 us)
Async XLA Ops:
  7.2 1.3 copy-start
  17.9 20.9 %all-to-all-start = ((s32[128,1,12]{2,1,0:T(1,128)}), s32[128,1,12]{2,1,0:T(1,128)S(1)}, u32[]{:S(2)}, u32[]{:S(2)}) async-start(s32[128,1,12]{2,1,0:T(1,128)} %bitcast.7), calls=%async_computation | async-start | bytes 131072 | tf_op jit(solution)/shard_map/all_to_all | solution.py:29
  51.4 58.4 %all-to-all-start.1 = ((f32[128,12,400]{2,1,0:T(8,128)}), f32[128,12,400]{2,1,0:T(8,128)}, u32[]{:S(2)}, u32[]{:S(2)}) async-start(f32[128,12,400]{2,1,0:T(8,128)} %reshape.313), calls=%async_computation.1 | async-start | bytes 8388608 | tf_op jit(solution)/shard_map/all_to_all | solution.py:33
  57.2 103.0 %all-gather.2.cloned.1.call-start = ((), (), s32[]{:S(2)}) async-start(), calls=%async_computation.4 | async-start | bytes 7372800 | tf_op jit(solution)/shard_map/all_gather | solution.py:71
  120.3 14.5 %copy-start.5 = (s32[128]{0:T(128)S(1)}, s32[128]{0:T(128)}, u32[]{:S(2)}) copy-start(s32[128]{0:T(128)} %param.13) | copy-start | bytes 1540
  120.4 100.7 %reduce-scatter.2.cloned.1.call-start = ((), (), s32[]{:S(2)}) async-start(), calls=%async_computation.5 | async-start | bytes 7372800 | tf_op jit(solution)/shard_map/reduce_scatter | solution.py:73
  160.2 4.7 %copy-start.3 = (f32[4096,400]{0,1:T(8,128)S(1)}, f32[4096,400]{0,1:T(8,128)}, u32[]{:S(2)}) copy-start(f32[4096,400]{0,1:T(8,128)} %all-gather.2.cloned.1.call-done) | copy-start | bytes 19660804
  236.5 61.4 %all-to-all-start.2 = ((f32[128,12,400]{2,1,0:T(8,128)}), f32[128,12,400]{2,1,0:T(8,128)}, u32[]{:S(2)}, u32[]{:S(2)}) async-start(f32[128,12,400]{2,1,0:T(8,128)} %reshape.302), calls=%async_computation.3 | async-start | bytes 8388608 | tf_op jit(solution)/shard_map/all_to_all | solution.py:33
  314.9 2.7 copy-start.4
  314.9 3.5 %copy-start.2 = (f32[2048,400]{1,0:T(8,128)S(1)}, f32[2048,400]{1,0:T(8,128)}, u32[]{:S(2)}) copy-start(f32[2048,400]{1,0:T(8,128)} %copy.39) | copy-start | bytes 9830404
  318.4 10.1 %copy-start.1 = (s32[262144]{0:T(1024)S(1)}, s32[262144]{0:T(1024)}, u32[]{:S(2)}) copy-start(s32[262144]{0:T(1024)} %param.11) | copy-start | bytes 3145732
Sparse Core Ops, SparseCore 0:
  120.5 39.7 all-gather.1
  178.3 42.7 reduce-scatter.1
where the time goes:
time: 337 us; the launch traced here: 335 us
  waiting for transfers between devices  162 us (48%)
  local copies, waits for them, and re-layouts  84.3 us (25%)
  other arithmetic  28 us (8%)
  starting transfers between devices  26.5 us (8%)
  matrix products  20.8 us (6%)
  between operations  14.3 us (4%)
    all_to_all x2, waiting for transfers between devices, move_rows(): lax.all_to_all(payload, ('dp', 'blk'), split_axis=0, concat_axis=0, tiled...  104 us
    reduce_scatter x1, waiting for transfers between devices, on_device(): lax.psum_scatter(part_block, 'blk', scatter_dimension=0, tiled=True)  35.3 us
    unnamed x18, local copies, waits for them, and re-layouts  27.6 us
    all_gather x1, waiting for transfers between devices, on_device(): lax.all_gather(neg_block, 'blk', axis=0, tiled=True)  18.3 us
    all_to_all x2, starting transfers between devices, move_rows(): lax.all_to_all(payload, ('dp', 'blk'), split_axis=0, concat_axis=0, tiled...  14.7 us
    gather x2, local copies, waits for them, and re-layouts, on_device(): served = entity_table[asked_rows]  12.4 us
    scatter-add x1, other arithmetic, on_device(): jnp.zeros_like(entity_table).at[asked_rows.reshape(-1)]  12.4 us
    all_to_all x1, starting transfers between devices, send_requests(): lax.all_to_all(requests, ('dp', 'blk'), split_axis=0, concat_axis=0, tile...  11.5 us
  transfers between devices with their start and end apart: 5, of which 5 were waited for; matrix products, arithmetic and copies ran while one was open for 11% of the time, Pallas kernels for 0%

commit v1 on v0

--- a/solution.py
+++ b/solution.py
@@ -68,7 +68,11 @@
     grad_pos = (jax.nn.sigmoid(pos_dist - MARGIN) / pos_dist)[:, None] * residue
     weight = float(blk_count * neg_count)
     part_query, part_block = negative_terms(
-        queries, lax.all_gather(neg_block, "blk", axis=0, tiled=True), weight
+        queries,
+        jnp.concatenate(
+            lax.all_to_all(jnp.stack([neg_block] * lax.axis_size("blk")), "blk", 0, 0), axis=0
+        ),
+        weight,
     )
     block_grad = lax.psum_scatter(part_block, "blk", scatter_dimension=0, tiled=True)
     gradients = jnp.concatenate([grad_pos + part_query, -grad_pos, block_grad])

time: 337 us -> 381 us (1.13)
  waiting for transfers between devices: 162 us -> 193 us
  starting transfers between devices: 26.5 us -> 32.1 us
  local copies, waits for them, and re-layouts: 84.3 us -> 89.1 us
    all_to_all x0 -> x1, waiting for transfers between devices: none -> 53.3 us  [on_device(): lax.all_to_all(jnp.stack([neg_block] * lax.axis_size('blk')), 'blk', 0, 0)]
    all_gather x1 -> x0, waiting for transfers between devices: 18.3 us -> none  [on_device(): lax.all_gather(neg_block, 'blk', axis=0, tiled=True)]
    all_to_all x0 -> x1, starting transfers between devices: none -> 5.91 us  [on_device(): lax.all_to_all(jnp.stack([neg_block] * lax.axis_size('blk')), 'blk', 0, 0)]
  transfers between devices with their start and end apart: 5 -> 5, of which waited for: 5 -> 5; matrix products, arithmetic and copies ran while one was open for 11% -> 9% of each run, Pallas kernels for 0% -> 0%
where the time goes in v1:
time: 381 us; the launch traced here: 380 us
  waiting for transfers between devices  193 us (51%)
  local copies, waits for them, and re-layouts  89.1 us (23%)
  starting transfers between devices  32.1 us (8%)
  other arithmetic  30.4 us (8%)
  matrix products  20.8 us (5%)
  between operations  14.3 us (4%)
    all_to_all x2, waiting for transfers between devices, move_rows(): lax.all_to_all(payload, ('dp', 'blk'), split_axis=0, concat_axis=0, tiled...  104 us
    all_to_all x1, waiting for transfers between devices, on_device(): lax.all_to_all(jnp.stack([neg_block] * lax.axis_size('blk')), 'blk', 0, 0)  53.3 us
    reduce_scatter x1, waiting for transfers between devices, on_device(): lax.psum_scatter(part_block, 'blk', scatter_dimension=0, tiled=True)  32.1 us
    unnamed x18, local copies, waits for them, and re-layouts  25.1 us
    all_to_all x2, starting transfers between devices, move_rows(): lax.all_to_all(payload, ('dp', 'blk'), split_axis=0, concat_axis=0, tiled...  14.6 us
    gather x2, local copies, waits for them, and re-layouts, on_device(): served = entity_table[asked_rows]  12.4 us
    scatter-add x1, other arithmetic, on_device(): jnp.zeros_like(entity_table).at[asked_rows.reshape(-1)]  12.4 us
    all_to_all x1, starting transfers between devices, send_requests(): lax.all_to_all(requests, ('dp', 'blk'), split_axis=0, concat_axis=0, tile...  11.5 us
  transfers between devices with their start and end apart: 5, of which 5 were waited for; matrix products, arithmetic and copies ran while one was open for 9% of the time, Pallas kernels for 0%

profile of v1, /device:TPU:1, one launch (start us, length us, event | category | flops | bytes accessed | tf_op | source)
XLA Modules:
  0.0 380.0 jit_solution(3929962567320525594)
XLA Ops:
  7.2 0.8 fusion.20
  8.0 0.4 copy-done
  8.4 4.5 %gather_fusion = s32[768]{0:T(1024)S(1)} fusion(s32[262144]{0:T(1024)S(1)} %copy-done, s32[1024]{0:T(1024)S(1)} %pad_clamp_fusion.3), kind=kCustom, calls=%fused_computation | custom fusion | bytes 9216 | tf_op jit(solution)/shard_map/gather | solution.py:48
  12.9 0.1 copy.29
  13.1 0.2 fusion.8
  13.4 0.3 fusion.11
  13.8 3.4 scatter_custom_fusion
  17.2 0.7 all_to_all.17
  17.9 11.5 %all-to-all-start = ((s32[128,1,12]{2,1,0:T(1,128)}), s32[128,1,12]{2,1,0:T(1,128)S(1)}, u32[]{:S(2)}, u32[]{:S(2)}) async-start(s32[128,1,12]{2,1,0:T(1,128)} %bitcast.7), calls=%async_computation | async-start | bytes 131072 | tf_op jit(solution)/shard_map/all_to_all | solution.py:29
  29.4 5.0 %copy.40 = f32[2048,400]{1,0:T(8,128)} copy(f32[2048,400]{0,1:T(8,128)} %param.8) | data formatting | bytes 6553600 | tf_op args[0]
  34.4 4.4 %all-to-all-done = s32[128,1,12]{2,1,0:T(1,128)S(1)} async-done(((s32[128,1,12]{2,1,0:T(1,128)}), s32[128,1,12]{2,1,0:T(1,128)S(1)}, u32[]{:S(2)}, u32[]{:S(2)}) %all-to-all-start) | async-done | bytes 6176 | tf_op jit(solution)/shard_map/all_to_all | solution.py:29
  38.9 7.9 %gather_fusion.1 = f32[1536,400]{1,0:T(8,128)} fusion(f32[2048,400]{1,0:T(8,128)} %copy.40, s32[2048]{0:T(1024)S(1)} %pad_clamp_fusion), kind=kCustom, calls=%fused_computation.1 | custom fusion | bytes 4921344 | tf_op jit(solution)/shard_map/gather | solution.py:60
  46.8 4.6 %reshape.321 = f32[128,12,400]{2,1,0:T(8,128)} reshape(f32[1536,400]{1,0:T(8,128)} %gather_fusion.1) | data formatting | bytes 4915200 | tf_op jit(solution)/shard_map/gather | solution.py:60
  51.4 5.8 %all-to-all-start.1 = ((f32[128,12,400]{2,1,0:T(8,128)}), f32[128,12,400]{2,1,0:T(8,128)}, u32[]{:S(2)}, u32[]{:S(2)}) async-start(f32[128,12,400]{2,1,0:T(8,128)} %reshape.321), calls=%async_computation.1 | async-start | bytes 8388608 | tf_op jit(solution)/shard_map/all_to_all | solution.py:33
  57.2 52.5 %all-to-all-done.1 = f32[128,12,400]{2,1,0:T(8,128)} async-done(((f32[128,12,400]{2,1,0:T(8,128)}), f32[128,12,400]{2,1,0:T(8,128)}, u32[]{:S(2)}, u32[]{:S(2)}) %all-to-all-start.1) | async-done | bytes 2457632 | tf_op jit(solution)/shard_map/all_to_all | solution.py:33
  109.7 4.6 %reshape.308 = f32[1536,400]{1,0:T(8,128)} reshape(f32[128,12,400]{2,1,0:T(8,128)} %all-to-all-done.1) | data formatting | bytes 4915200 | tf_op jit(solution)/shard_map/reshape | solution.py:61
  114.3 4.7 %gather_fusion.2 = f32[768,400]{1,0:T(8,128)S(1)} fusion(f32[1536,400]{1,0:T(8,128)} %reshape.308, s32[1024]{0:T(1024)S(1)} %pad_clamp_fusion.2), kind=kCustom, calls=%fused_computation.2 | custom fusion | bytes 2460672 | tf_op jit(solution)/shard_map/gather | solution.py:61
  119.1 0.3 copy.37
  119.4 3.6 stack.2
  123.0 5.9 %all-to-all-start.2 = ((f32[8,512,400]{1,2,0:T(8,128)}), f32[8,512,400]{1,2,0:T(8,128)}, u32[]{:S(2)}, u32[]{:S(2)}) async-start(f32[8,512,400]{1,2,0:T(8,128)} %stack.2), calls=%async_computation.2 | async-start | bytes 13107200 | tf_op jit(solution)/shard_map/all_to_all | solution.py:73
  128.9 14.1 %copy.34 = f32[7424,400]{1,0:T(8,128)} copy(f32[7424,400]{0,1:T(8,128)} %param.10) | data formatting | bytes 23756800 | tf_op args[2]
  143.1 6.2 %gather_fusion.3 = f32[128,400]{1,0:T(8,128)S(1)} fusion(f32[7424,400]{1,0:T(8,128)} %copy.34, s32[1024]{0:T(1024)S(1)} %pad_clamp_fusion.1), kind=kCustom, calls=%fused_computation.3 | custom fusion | bytes 410112 | tf_op jit(solution)/shard_map/gather | solution.py:65
  149.3 0.1 copy.35
  149.4 0.1 copy.42
  149.6 0.1 copy.43
  149.8 53.3 %all-to-all-done.2 = f32[8,512,400]{1,2,0:T(8,128)} async-done(((f32[8,512,400]{1,2,0:T(8,128)}), f32[8,512,400]{1,2,0:T(8,128)}, u32[]{:S(2)}, u32[]{:S(2)}) %all-to-all-start.2) | async-done | bytes 6553632 | tf_op jit(solution)/shard_map/all_to_all | solution.py:73
  203.1 3.6 copy.44
  206.8 6.1 %multiply_reduce_fusion = f32[8,512]{1,0:T(8,128)S(1)} fusion(f32[8,512,400]{1,2,0:T(8,128)} %all-to-all-done.2), kind=kLoop, calls=%fused_computation.8 | loop fusion | flops 3272704 | bytes 6569984 | tf_op jit(solution)/shard_map/reduce_sum | solution.py:13
  212.9 5.5 %fusion.23 = (f32[128]{0:T(128)S(1)}, f32[4096]{0:T(1024)S(1)}, f32[128,4096]{1,0:T(8,128)S(1)}) fusion(f32[128,400]{0,1:T(8,128)S(1)} %get-tuple-element.12, f32[4096,400]{0,1:T(8,128)S(1)} %bitcast.44, f32[4096]{0:T(1024)S(1)} %bitcast.50, f32[128]{0:T(128)S(1)} %multiply_reduce_fusion.2), kind=kOutput, calls=%fused_computation.73 | convolution fusion | flops 2523394048 | bytes 8889344 | tf_op jit(solution)/shard_map/dot_general | solution.py:14
  218.4 7.6 %multiply_subtract_fusion = f32[4096,400]{0,1:T(8,128)} fusion(f32[4096,400]{0,1:T(8,128)S(1)} %bitcast.45, f32[128,4096]{1,0:T(8,128)S(1)} %get-tuple-element.17, f32[128,400]{0,1:T(8,128)S(1)} %get-tuple-element.12, f32[4096]{0:T(1024)S(1)} %get-tuple-element.7), kind=kOutput, calls=%fused_computation.7 | convolution fusion | flops 2519859200 | bytes 15425536 | tf_op jit(solution)/shard_map/dot_general | solution.py:22
  226.1 7.6 %fusion.7 = f32[128,400]{0,1:T(8,128)S(1)} fusion(f32[128,4096]{1,0:T(8,128)S(1)} %get-tuple-element.17, f32[4096,400]{0,1:T(8,128)} %bitcast.46, f32[128,400]{0,1:T(8,128)S(1)} %get-tuple-element.12, f32[128,400]{0,1:T(8,128)S(1)} %get-tuple-element.11, f32[128]{0:T(128)S(1)} %get-tuple-element.6, f32[128]{0:T(128)S(1)} %multiply_divide_fusion.1), kind=kOutput, calls=%fused_computation.22 | convolution fusion | flops 2516787200 | bytes 9266176 | tf_op jit(solution)/shard_map/dot_general | solution.py:19
  233.7 32.1 %reduce-scatter.2.cloned.1.call-done = f32[512,400]{0,1:T(8,128)} async-done(((f32[4096,400]{0,1:T(8,128)}), f32[512,400]{0,1:T(8,128)}) %reduce-scatter.2.cloned.1.call-update) | async-done | bytes 819216 | tf_op jit(solution)/shard_map/reduce_scatter | solution.py:77
  265.8 1.2 pad_maximum_fusion
  267.0 1.6 copy.39
  268.7 8.0 %scatter_custom_fusion.1 = f32[1536,400]{1,0:T(8,128)} fusion(s32[768]{0:T(1024)S(1)} %fusion.21, f32[768,400]{1,0:T(8,128)} %copy.39, f32[]{:T(128)} %constant.21.clone.1), kind=kCustom, calls=%fused_computation.18 | custom fusion | bytes 2458112 | tf_op jit(solution)/shard_map/scatter | solution.py:79
  276.7 4.6 %reshape.310 = f32[128,12,400]{2,1,0:T(8,128)} reshape(f32[1536,400]{1,0:T(8,128)} %scatter_custom_fusion.1) | data formatting | bytes 4915200 | tf_op jit(solution)/shard_map/reshape | solution.py:80
  281.2 8.9 %all-to-all-start.3 = ((f32[128,12,400]{2,1,0:T(8,128)}), f32[128,12,400]{2,1,0:T(8,128)}, u32[]{:S(2)}, u32[]{:S(2)}) async-start(f32[128,12,400]{2,1,0:T(8,128)} %reshape.310), calls=%async_computation.4 | async-start | bytes 8388608 | tf_op jit(solution)/shard_map/all_to_all | solution.py:33
  290.1 0.5 broadcast.248
  290.6 0.8 reduce.10
  291.4 0.1 reshape.307
  291.6 51.1 %all-to-all-done.3 = f32[128,12,400]{2,1,0:T(8,128)} async-done(((f32[128,12,400]{2,1,0:T(8,128)}), f32[128,12,400]{2,1,0:T(8,128)}, u32[]{:S(2)}, u32[]{:S(2)}) %all-to-all-start.3) | async-done | bytes 2457632 | tf_op jit(solution)/shard_map/all_to_all | solution.py:33
  342.6 4.6 %reshape.364 = f32[1536,400]{1,0:T(8,128)} reshape(f32[128,12,400]{2,1,0:T(8,128)} %all-to-all-done.3) | data formatting | bytes 4915200 | tf_op jit(solution)/shard_map/reshape | solution.py:82
  347.2 12.4 %scatter_custom_fusion.2 = f32[2048,400]{1,0:T(8,128)} fusion(s32[1536]{0:T(1024)S(1)} %fusion.13, f32[1536,400]{1,0:T(8,128)} %reshape.364, f32[]{:T(128)} %constant.21.clone.1), kind=kCustom, calls=%fused_computation.16 | custom fusion | flops 614400 | bytes 3277312 | tf_op jit(solution)/shard_map/scatter-add | solution.py:82
  359.6 2.7 multiply_reduce_fusion.1
  362.3 0.6 fusion.24
  362.9 0.1 copy-done.2
  363.1 4.9 %divide_subtract_fusion = f32[2048,400]{1,0:T(8,128)} fusion(f32[2048,400]{1,0:T(8,128)S(1)} %copy-done.2, f32[2048,400]{1,0:T(8,128)} %scatter_custom_fusion.2, f32[2048]{0:T(1024)S(1)} %get-tuple-element.8), kind=kLoop, calls=%fused_computation.13 | loop fusion | flops 2457600 | bytes 9838592 | tf_op jit(solution)/shard_map/sub | solution.py:85
  368.0 5.2 %copy.41 = f32[2048,400]{0,1:T(8,128)} copy(f32[2048,400]{1,0:T(8,128)} %divide_subtract_fusion) | data formatting | bytes 6553600
  (34 shorter events, 0.7 us)
Async XLA Ops:
  7.2 1.3 copy-start
  17.9 20.9 %all-to-all-start = ((s32[128,1,12]{2,1,0:T(1,128)}), s32[128,1,12]{2,1,0:T(1,128)S(1)}, u32[]{:S(2)}, u32[]{:S(2)}) async-start(s32[128,1,12]{2,1,0:T(1,128)} %bitcast.7), calls=%async_computation | async-start | bytes 131072 | tf_op jit(solution)/shard_map/all_to_all | solution.py:29
  51.4 58.3 %all-to-all-start.1 = ((f32[128,12,400]{2,1,0:T(8,128)}), f32[128,12,400]{2,1,0:T(8,128)}, u32[]{:S(2)}, u32[]{:S(2)}) async-start(f32[128,12,400]{2,1,0:T(8,128)} %reshape.321), calls=%async_computation.1 | async-start | bytes 8388608 | tf_op jit(solution)/shard_map/all_to_all | solution.py:33
  123.0 80.1 %all-to-all-start.2 = ((f32[8,512,400]{1,2,0:T(8,128)}), f32[8,512,400]{1,2,0:T(8,128)}, u32[]{:S(2)}, u32[]{:S(2)}) async-start(f32[8,512,400]{1,2,0:T(8,128)} %stack.2), calls=%async_computation.2 | async-start | bytes 13107200 | tf_op jit(solution)/shard_map/all_to_all | solution.py:73
  128.9 14.1 %copy-start.5 = (s32[128]{0:T(128)S(1)}, s32[128]{0:T(128)}, u32[]{:S(2)}) copy-start(s32[128]{0:T(128)} %param.13) | copy-start | bytes 1540
  128.9 136.9 %reduce-scatter.2.cloned.1.call-start = ((), (), s32[]{:S(2)}) async-start(), calls=%async_computation.5 | async-start | bytes 7372800 | tf_op jit(solution)/shard_map/reduce_scatter | solution.py:77
  206.8 11.6 %copy-start.3 = (f32[8,50,8,512]{3,2,0,1:T(8,128)}, f32[8,50,8,512]{3,2,0,1:T(8,128)S(1)}, u32[]{:S(2)}) copy-start(f32[8,50,8,512]{3,2,0,1:T(8,128)S(1)} %copy.44) | copy-start | bytes 19660804
  281.2 61.4 %all-to-all-start.3 = ((f32[128,12,400]{2,1,0:T(8,128)}), f32[128,12,400]{2,1,0:T(8,128)}, u32[]{:S(2)}, u32[]{:S(2)}) async-start(f32[128,12,400]{2,1,0:T(8,128)} %reshape.310), calls=%async_computation.4 | async-start | bytes 8388608 | tf_op jit(solution)/shard_map/all_to_all | solution.py:33
  359.6 2.7 copy-start.4
  359.6 3.5 copy-start.2
  363.1 10.1 %copy-start.1 = (s32[262144]{0:T(1024)S(1)}, s32[262144]{0:T(1024)}, u32[]{:S(2)}) copy-start(s32[262144]{0:T(1024)} %param.11) | copy-start | bytes 3145732
Sparse Core Ops, SparseCore 0:
  226.2 39.5 reduce-scatter.1
